TPU v7x, 512 devices: a whole 4x4x16 slice. The times are simulated.
512 devices in a mesh: pair: 64 (over z, x), int: 8 (over y, core).
Axes of the slice: x: 4, y: 4, z: 16, core: 2. Of those that a mesh axis runs over, the one named last changes fastest.
Arguments:
- amps: bfloat16 [512, 64, 4096], P('pair', None, 'int'), may hold values from -6 to 6
- amp_mask: int32 [512, 64], P('pair'), may hold values 0 or 1
- integrals: bfloat16 [64, 4096, 4096], P('pair', None, 'int'), may hold values from -0.09375 to 0.09375
- block_mask: int32 [64], P('pair'), may hold values 0 or 1
- in_tiles: int32 [64], replicated, may hold values from 0 to 63, each once
- out_tiles: int32 [64], replicated, may hold values from 0 to 63, each once
- vir_energy: float32 [1024], replicated, may hold values from 0.5 to 3
- pair_energy: float32 [512], P('pair'), may hold values from -4 to -1
- dressing: bfloat16 [1024, 1024], P('pair'), may hold values from -0.1875 to 0.1875
Outputs:
- new_amps: bfloat16 [512, 64, 4096], P('pair', None, 'int')
Inputs may be any that keep to these rules, and one draw needn't show every extreme that they name: `in_tiles`: a permutation of the 64 tiles. `out_tiles`: a permutation of the 64 tiles.
All inputs are finite; a program needn't handle non-finite values. No bound on the sum of `amp_mask` or of `block_mask` on one device may be relied on, other than what follows from the above.
Results may differ from a plain program's by a relative error of at most 0.0038.
Values may be sent and summed in bfloat16 or wider, within the bound.
A program may use at most 64 MiB of HBM per device.

v0:
```python
import jax
import jax.numpy as jnp
from jax import lax
from jax.sharding import PartitionSpec as P

TILE = 64
VT = 16
WA = 4


def shards(
    amps, amp_mask, integrals, block_mask, in_tiles, out_tiles, vir_energy, pair_energy, dressing
):
    local_pairs, tile_count, share_size = amps.shape
    strip_rows = share_size // TILE
    int_index = lax.axis_index("int")
    masked = jnp.where(amp_mask[:, :, None] > 0, amps, jnp.zeros_like(amps))
    ordered = jnp.take(masked, in_tiles, axis=1)
    received = lax.all_to_all(ordered, "pair", split_axis=1, concat_axis=0, tiled=True)
    partial_value = jnp.einsum(
        "psk,sak->psa", received, integrals, preferred_element_type=jnp.float32
    )
    partial_value = partial_value * block_mask.astype(jnp.float32)[None, :, None]
    partial_value = lax.optimization_barrier(partial_value.astype(jnp.bfloat16)).astype(jnp.float32)
    summed = lax.psum(partial_value.astype(jnp.bfloat16), "int").astype(jnp.float32)
    own_share = lax.dynamic_slice_in_dim(summed, int_index * share_size, share_size, 2)
    returned = lax.all_to_all(
        own_share.astype(jnp.bfloat16), "pair", split_axis=0, concat_axis=1, tiled=True
    ).astype(own_share.dtype)
    slot_of = (
        jnp.zeros((tile_count,), jnp.int32)
        .at[out_tiles]
        .set(jnp.arange(tile_count, dtype=jnp.int32))
    )
    ladder_terms = jnp.take(returned, slot_of, axis=1)
    tile_rows = masked.reshape(local_pairs, WA, VT, strip_rows, TILE)
    tile_rows = jnp.transpose(tile_rows, (0, 1, 3, 2, 4)).reshape(
        local_pairs * WA * strip_rows, VT * TILE
    )
    running = jnp.dot(
        tile_rows,
        lax.all_gather(dressing, "pair", axis=0, tiled=True),
        preferred_element_type=jnp.float32,
    )
    running = running.reshape(local_pairs, WA, strip_rows, VT, TILE)
    cycle_terms = jnp.transpose(running, (0, 1, 3, 2, 4)).reshape(
        local_pairs, tile_count, share_size
    )
    energies = vir_energy.reshape(VT, TILE)
    own_energy = lax.dynamic_slice_in_dim(energies[:WA], int_index * strip_rows, strip_rows, 1)
    denominator = (
        pair_energy[:, None, None, None, None]
        - own_energy[None, :, None, :, None]
        - energies[None, None, :, None, :]
    )
    denominator = denominator.reshape(local_pairs, tile_count, share_size)
    updated = masked.astype(jnp.float32) + (ladder_terms + cycle_terms) / denominator
    return updated.astype(jnp.bfloat16)


def solution(mesh):
    in_specs = (
        P("pair", None, "int"),
        P("pair", None),
        P("pair", None, "int"),
        P("pair"),
        P(),
        P(),
        P(),
        P("pair"),
        P("pair", None),
    )
    out_specs = P("pair", None, "int")
    return jax.shard_map(shards, mesh=mesh, in_specs=in_specs, out_specs=out_specs, check_vma=False)
```

profile of v0, /device:TPU:16, one launch (start us, length us, event | category | flops | bytes accessed | tf_op | source)
XLA Modules:
  0.0 241.5 jit_solution(16358082051121928171)
XLA Ops:
  7.4 0.7 broadcast_compare_fusion
  8.1 0.1 copy.18
  8.2 0.7 compare_and_fusion
  8.8 0.7 compare_select_fusion
  9.5 1.4 copy_select_fusion
  10.9 0.6 gather_fusion
  11.5 0.9 select_bitcast_fusion
  12.4 18.6 %all-to-all-start = ((bf16[8,64,512]{2,0,1:T(8,128)(2,1)}), bf16[8,64,512]{2,0,1:T(8,128)(2,1)S(1)}, u32[]{:S(2)}, u32[]{:S(2)}) async-start(bf16[8,64,512]{2,0,1:T(8,128)(2,1)} %select_bitcast_fusion), calls=%async_computation | async-start | bytes 1048576 | tf_op jit(solution)/shard_map/all_to_all | solution.py:19
  31.0 0.0 all-reduce.2.cloned.1.call-start
  31.7 32.1 %all-to-all-done = bf16[8,64,512]{2,0,1:T(8,128)(2,1)S(1)} async-done(((bf16[8,64,512]{2,0,1:T(8,128)(2,1)}), bf16[8,64,512]{2,0,1:T(8,128)(2,1)S(1)}, u32[]{:S(2)}, u32[]{:S(2)}) %all-to-all-start) | async-done | bytes 524320 | tf_op jit(solution)/shard_map/all_to_all | solution.py:19
  63.8 6.5 %fusion = bf16[512,1,4096]{2,0,1:T(8,128)(2,1)} fusion(bf16[1,4096,512]{2,1,0:T(8,128)(2,1)} %param.11, f32[]{:T(128)} %bitcast.5, bf16[8,64,512]{2,0,1:T(8,128)(2,1)S(1)} %all-to-all-done), kind=kOutput, calls=%fused_computation.4 | convolution fusion | flops 2151677952 | bytes 8912900 | tf_op jit(solution)/shard_map/psk,sak->psa/dot_general | solution.py:20
  70.3 0.0 copy-start
  70.3 0.0 slice-start
  70.3 0.0 copy-start.1
  70.3 0.0 all-reduce.2.cloned.1.call-update
  70.4 0.0 all-gather.2.cloned.1.call-start
  70.4 0.5 all-gather.2.cloned.1.call-update
  70.9 75.6 %all-reduce.2.cloned.1.call-done = bf16[512,1,4096]{2,0,1:T(8,128)(2,1)} async-done(((bf16[512,1,4096]{2,0,1:T(8,128)(2,1)}), bf16[512,1,4096]{2,0,1:T(8,128)(2,1)}) %all-reduce.2.cloned.1.call-update) | async-done | bytes 4194320 | tf_op jit(solution)/shard_map/psum | solution.py:25
  146.6 1.1 convert_convert_fusion
  147.7 0.5 broadcast.65
  148.2 1.0 reduce
  149.2 1.0 reshape.101
  150.2 15.8 %all-to-all-start.1 = ((bf16[64,2,2048]{2,1,0:T(2,128)(2,1)}), bf16[64,2,2048]{2,1,0:T(2,128)(2,1)}, u32[]{:S(2)}, u32[]{:S(2)}) async-start(bf16[64,2,2048]{2,1,0:T(2,128)(2,1)} %reshape.101), calls=%async_computation.1 | async-start | bytes 1048576 | tf_op jit(solution)/shard_map/all_to_all | solution.py:27
  166.0 1.5 reshape.65
  167.5 0.0 copy-done
  167.5 0.1 sub.45
  167.6 0.0 slice-done
  167.6 0.1 slice.15
  167.7 0.1 constant_dynamic-slice_fusion
  167.7 0.0 copy-done.1
  167.7 0.1 broadcast_subtract_fusion
  167.8 0.3 sub.43
  168.1 0.5 sub.44
  168.6 2.4 %copy.21 = bf16[8,4,8,16,64]{4,3,2,1,0:T(8,128)(2,1)S(1)} copy(bf16[8,4,8,16,64]{4,2,0,3,1:T(8,128)(2,1)} %bitcast.60) | data formatting | bytes 1048576 | tf_op jit(solution)/shard_map/transpose | solution.py:37
  171.1 1.5 reshape.96
  172.6 0.1 sub.47
  172.7 1.0 scatter_custom_fusion
  173.7 42.3 %all-gather.2.cloned.1.call-done = bf16[1024,1024]{1,0:T(8,128)(2,1)} async-done(((bf16[16,1024]{1,0:T(8,128)(2,1)}), bf16[1024,1024]{1,0:T(8,128)(2,1)}) %all-gather.2.cloned.1.call-update) | async-done | bytes 2097168 | tf_op jit(solution)/shard_map/all_gather | solution.py:42
  216.0 2.9 %copy.22 = bf16[1024,1024]{1,0:T(8,128)(2,1)S(1)} copy(bf16[1024,1024]{0,1:T(8,128)(2,1)} %bitcast.61) | data formatting | bytes 4194304 | tf_op jit(solution)/shard_map/dot_general | solution.py:40
  218.9 3.7 %convolution_bitcast_fusion = f32[8,4,16,8,64]{4,3,2,1,0:T(8,128)} fusion(bf16[16,64,1024,1,1]{2,1,0,4,3:T(8,128)(2,1)S(1)} %bitcast.62, bf16[8,4,8,1024,1]{3,2,1,0,4:T(8,128)(2,1)} %reshape.96), kind=kOutput, calls=%fused_computation.6 | convolution fusion | flops 536870912 | bytes 3670016 | tf_op jit(solution)/shard_map/dot_general | solution.py:40
  222.6 1.9 reshape.66
  224.5 0.0 all-to-all-done.1
  224.5 3.6 %reshape.102 = bf16[512,1,512]{2,1,0:T(2,128)(2,1)S(1)} reshape(bf16[64,2,2048]{2,1,0:T(2,128)(2,1)} %all-to-all-done.1) | data formatting | bytes 1048576
  228.1 1.1 copy.33
  229.2 1.8 gather_fusion.1
  231.1 2.1 fusion.4
  233.1 0.9 copy.24
  (6 shorter events, 0.0 us)
Async XLA Ops:
  12.4 51.4 %all-to-all-start = ((bf16[8,64,512]{2,0,1:T(8,128)(2,1)}), bf16[8,64,512]{2,0,1:T(8,128)(2,1)S(1)}, u32[]{:S(2)}, u32[]{:S(2)}) async-start(bf16[8,64,512]{2,0,1:T(8,128)(2,1)} %select_bitcast_fusion), calls=%async_computation | async-start | bytes 1048576 | tf_op jit(solution)/shard_map/all_to_all | solution.py:19
  31.0 115.6 %all-reduce.2.cloned.1.call-start = ((), (), s32[]{:S(2)}) async-start(), calls=%async_computation.2 | async-start | bytes 8388608 | tf_op jit(solution)/shard_map/psum | solution.py:25
  70.3 97.2 %copy-start = (f32[1024]{0:T(1024)S(1)}, f32[1024]{0:T(1024)}, u32[]{:S(2)}) copy-start(f32[1024]{0:T(1024)} %param.15) | copy-start | bytes 12292
  70.3 97.3 %slice-start = ((f32[1024]{0:T(1024)}), f32[256]{0:T(256)S(1)}, s32[]{:S(2)}) async-start(f32[1024]{0:T(1024)} %param.15), calls=%async_computation.4 | async-start | bytes 2048 | tf_op jit(solution)/shard_map/slice | solution.py:50
  70.3 97.4 %copy-start.1 = (f32[8]{0:T(128)S(1)}, f32[8]{0:T(128)}, u32[]{:S(2)}) copy-start(f32[8]{0:T(128)} %param.16) | copy-start | bytes 100
  70.4 145.7 %all-gather.2.cloned.1.call-start = ((), (), s32[]{:S(2)}) async-start(), calls=%async_computation.3 | async-start | bytes 2129920 | tf_op jit(solution)/shard_map/all_gather | solution.py:42
  150.2 74.3 %all-to-all-start.1 = ((bf16[64,2,2048]{2,1,0:T(2,128)(2,1)}), bf16[64,2,2048]{2,1,0:T(2,128)(2,1)}, u32[]{:S(2)}, u32[]{:S(2)}) async-start(bf16[64,2,2048]{2,1,0:T(2,128)(2,1)} %reshape.101), calls=%async_computation.1 | async-start | bytes 1048576 | tf_op jit(solution)/shard_map/all_to_all | solution.py:27
Sparse Core Ops, SparseCore 0:
  70.5 76.0 all-reduce.1
Sparse Core Ops, SparseCore 1:
  73.8 142.2 all-gather.1
where the time goes:
time: 242 us
  waiting for transfers between devices  151 us (62%)
  starting transfers between devices  34.4 us (14%)
  local copies, waits for them, and re-layouts  22.1 us (9%)
  between operations  15.6 us (6%)
  matrix products  10.2 us (4%)
  other arithmetic  8.61 us (4%)
    psum x1, waiting for transfers between devices, shards(): lax.psum(partial_value.astype(jnp.bfloat16), 'int').astype(jnp.float32)  75.6 us
    all_gather x1, waiting for transfers between devices, shards(): lax.all_gather(dressing, 'pair', axis=0, tiled=True)  42.3 us
    all_to_all x1, waiting for transfers between devices, shards(): lax.all_to_all(ordered, 'pair', split_axis=1, concat_axis=0, tiled=True)  32.1 us
    all_to_all x1, starting transfers between devices, shards(): lax.all_to_all(ordered, 'pair', split_axis=1, concat_axis=0, tiled=True)  18.6 us
    all_to_all x1, starting transfers between devices, shards(): lax.all_to_all(own_share.astype(jnp.bfloat16), 'pair', split_axis=0, conc...  15.8 us
    dot_general x1, matrix products, shards(): jnp.einsum('psk,sak->psa', received, integrals, preferred_element_type=jn...  6.51 us
    unnamed x7, local copies, waits for them, and re-layouts  5.7 us
  transfers between devices with their start and end apart: 4, of which 3 were waited for; matrix products, arithmetic and copies ran while one was open for 8% of the time, Pallas kernels for 0%

commit v1 on v0

v1 whole, which is shorter than its diff:
```python
import functools

import jax
import jax.numpy as jnp
from jax import lax
from jax.experimental import pallas as pl
from jax.experimental.pallas import tpu as pltpu
from jax.sharding import PartitionSpec as P

MESH = pl.DeviceIdType.MESH
BF16 = jnp.bfloat16
F32 = jnp.float32
WA = 4
NX = 4
LANES = 128
NC = 2
CUTS = (0, 44, 64)


def kernel(
    cuts,
    amps_ref,
    mask_ref,
    ints_hbm,
    block_s,
    in_s,
    slot_s,
    energy_s,
    energy_ref,
    pair_energy_s,
    dress_ref,
    out_ref,
    ints,
    amps32,
    asend,
    arecv,
    rows,
    psend,
    precv,
    own,
    ysend,
    yrecv,
    dsend,
    drecv,
    gathered,
    dress,
    lhs,
    cycle,
    ladder,
    first_energy,
    second_energy,
    ints_sem,
    a_send,
    a_recv,
    p_send,
    p_recv,
    y_send,
    y_recv,
    d_send,
    d_recv,
    g_send,
    g_recv,
):
    npair = asend.shape[0]
    pairs, tiles, share = amps_ref.shape
    nz = npair // NX
    nint, _, _, _, band = gathered.shape
    ny = nint // NC
    vt = tiles // WA
    chunks = len(cuts) - 1
    blocks = share // LANES
    n, i = lax.axis_index("pair"), lax.axis_index("int")
    z, x = lax.div(n, NX), lax.rem(n, NX)
    y, c = lax.div(i, NC), lax.rem(i, NC)

    def peer(o, sign):
        zi, dx = lax.div(o, NX), lax.rem(o, NX)
        half = lax.div(zi + 1, 2)
        dz = jnp.where(lax.rem(zi, 2) == 1, half, nz - half)
        zz = lax.rem(z + nz + sign * dz + nz, nz)
        xx = lax.rem(x + NX + sign * dx, NX)
        return zz * NX + xx

    def y_peer(dy):
        return lax.rem(y + dy, ny) * NC + c

    partner = y * NC + (1 - c)

    barrier = pltpu.get_barrier_semaphore()

    def greet(o, carry):
        pl.semaphore_signal(barrier, 1, device_id={"pair": peer(o, 1)}, device_id_type=MESH)
        return carry

    lax.fori_loop(1, npair, greet, 0)
    pl.semaphore_signal(barrier, 1, device_id={"int": partner}, device_id_type=MESH)
    for dy in range(1, ny):
        pl.semaphore_signal(barrier, 1, device_id={"int": y_peer(dy)}, device_id_type=MESH)

    load_ints = pltpu.make_async_copy(ints_hbm.at[0], ints, ints_sem)
    load_ints.start()

    mask_t = jnp.transpose(mask_ref[...].astype(F32))
    for p in range(pairs):
        keep = jnp.broadcast_to(mask_t[:, p : p + 1], (tiles, share)) > 0
        kept = jnp.where(keep, amps_ref[p].astype(F32), 0.0)
        for b in range(blocks):
            amps32[b, p * tiles : (p + 1) * tiles, :] = kept[:, b * LANES : (b + 1) * LANES]

    def order(o, carry):
        t = in_s[peer(o, 1)]
        for b in range(blocks):
            asend[o, :, b * LANES : (b + 1) * LANES] = amps32[b, pl.ds(t, pairs, stride=tiles), :].astype(BF16)
        return carry

    lax.fori_loop(0, npair, order, 0)
    arecv[0] = asend[0]

    pl.semaphore_wait(barrier, npair - 1 + 1 + ny - 1)

    def a_copy(k, o):
        return pltpu.make_async_remote_copy(
            asend.at[o], arecv.at[o], a_send.at[k], a_recv.at[k],
            device_id={"pair": peer(o, 1)}, device_id_type=MESH)

    def many(src, dst, ssem, rsem, k):
        first, last = max(cuts[k], 1), cuts[k + 1]
        return pltpu.make_async_remote_copy(
            src.at[pl.ds(first, last - first)], dst.at[pl.ds(first, last - first)],
            ssem.at[k], rsem.at[k], device_id={"pair": peer(1, 1)}, device_id_type=MESH)

    for k in range(chunks):
        def start_a(o, carry, k=k):
            a_copy(k, o).start()
            return carry
        lax.fori_loop(max(cuts[k], 1), cuts[k + 1], start_a, 0)

    piece = dress_ref.at[:, pl.ds(pl.multiple_of(i * band, band), band)]
    own_piece = pltpu.make_async_copy(piece, gathered.at[i, x, z], g_send.at[0])
    own_piece.start()
    own_piece.wait()

    def g_z_copy(dz):
        return pltpu.make_async_remote_copy(
            piece, gathered.at[i, x, z], g_send.at[1], g_recv.at[1],
            device_id={"pair": lax.rem(z + dz, nz) * NX + x}, device_id_type=MESH)

    def g_x_copy(dx):
        return pltpu.make_async_remote_copy(
            gathered.at[i, x], gathered.at[i, x], g_send.at[2], g_recv.at[2],
            device_id={"pair": z * NX + lax.rem(x + dx, NX)}, device_id_type=MESH)

    def g_y_copy(dy):
        return pltpu.make_async_remote_copy(
            gathered.at[i], gathered.at[i], g_send.at[3], g_recv.at[3],
            device_id={"int": y_peer(dy)}, device_id_type=MESH)

    def g_c_copy(yy):
        return pltpu.make_async_remote_copy(
            gathered.at[yy * NC + c], gathered.at[yy * NC + c], g_send.at[4], g_recv.at[4],
            device_id={"int": partner}, device_id_type=MESH)

    def start_gz(dz, carry):
        g_z_copy(dz).start()
        return carry

    lax.fori_loop(1, nz, start_gz, 0)

    def drain(ref, ssem, rsem):
        copy = pltpu.make_async_remote_copy(
            ref, ref, ssem, rsem, device_id={"int": partner}, device_id_type=MESH)
        copy.wait_send()
        copy.wait_recv()

    low = lax.broadcasted_iota(jnp.int32, (1, 128), 1) < 64
    count = pairs * WA
    for j in range(vt // 2):
        for ap in range(blocks):
            even = amps32[ap, pl.ds(2 * j, count, stride=vt), :]
            odd = amps32[ap, pl.ds(2 * j + 1, count, stride=vt), :]
            at = ap * count
            lhs[at : at + count, j * 128 : (j + 1) * 128] = jnp.where(
                low, even, pltpu.roll(odd, 64, 1)).astype(BF16)
            at += blocks * count
            lhs[at : at + count, j * 128 : (j + 1) * 128] = jnp.where(
                low, pltpu.roll(even, 64, 1), odd).astype(BF16)

    energies = energy_ref[...]
    turned = pltpu.roll(energies, 64, 1)
    for j in range(vt // 2):
        spread = jnp.where(low, energies[j : j + 1], turned[j : j + 1])
        second_energy[2 * j : 2 * j + 1, :] = jnp.concatenate([spread] * (share // 128), 1)
        spread = jnp.where(low, turned[j : j + 1], energies[j : j + 1])
        second_energy[2 * j + 1 : 2 * j + 2, :] = jnp.concatenate([spread] * (share // 128), 1)
    strip = lax.broadcasted_iota(jnp.int32, (1, share), 1) // 64
    for a in range(WA):
        row = jnp.zeros((1, share), F32)
        for s in range(share // 64):
            row = jnp.where(strip == s, energy_s[64 * a + i * (share // 64) + s], row)
        first_energy[a : a + 1, :] = row

    scale = block_s[0].astype(F32)
    load_ints.wait()

    def product(r0, rn, j):
        block = ints[pl.ds(pl.multiple_of(j * share, share), share), :]
        part = lax.dot_general(
            rows[r0 : r0 + rn, :], block, (((1,), (1,)), ((), ())), preferred_element_type=F32)
        return (part * scale).astype(BF16)

    def p_copy(k, yy):
        span = pl.ds(cuts[k] * pairs, (cuts[k + 1] - cuts[k]) * pairs)
        return pltpu.make_async_remote_copy(
            psend.at[yy, span], precv.at[yy, span], p_send.at[k, yy], p_recv.at[k, yy],
            device_id={"int": partner}, device_id_type=MESH)

    def y_copy(k, dy):
        span = pl.ds(cuts[k] * pairs, (cuts[k + 1] - cuts[k]) * pairs)
        return pltpu.make_async_remote_copy(
            ysend.at[dy - 1, span], yrecv.at[dy - 1, span], y_send.at[k, dy - 1], y_recv.at[k, dy - 1],
            device_id={"int": y_peer(dy)}, device_id_type=MESH)

    def multiply(k):
        o0, o1 = cuts[k], cuts[k + 1]
        r0, rn = o0 * pairs, (o1 - o0) * pairs
        many(asend, arecv, a_send, a_recv, k).wait_recv()
        rows[r0 : r0 + rn, :] = arecv[o0:o1].astype(F32).reshape(rn, share).astype(BF16)

        def for_partner(yy, carry):
            psend[yy, r0 : r0 + rn, :] = product(r0, rn, yy * NC + 1 - c)
            p_copy(k, yy).start()
            return carry

        lax.fori_loop(0, ny, for_partner, 0)

        def for_chip(step, carry):
            dy = ny - 1 - step
            yy = lax.rem(y + dy, ny)
            part = product(r0, rn, yy * NC + c).astype(F32)
            p_copy(k, yy).wait_recv()
            part = part + precv[yy, r0 : r0 + rn, :].astype(F32)

            @pl.when(dy > 0)
            def _():
                ysend[dy - 1, r0 : r0 + rn, :] = part.astype(BF16)
                y_copy(k, dy).start()

            @pl.when(dy == 0)
            def _():
                own[r0 : r0 + rn, :] = part

            return carry

        lax.fori_loop(0, ny, for_chip, 0)

    def d_copy(k, o):
        return pltpu.make_async_remote_copy(
            dsend.at[o], drecv.at[o], d_send.at[k], d_recv.at[k],
            device_id={"pair": peer(o, -1)}, device_id_type=MESH)

    def finish(k):
        o0, o1 = cuts[k], cuts[k + 1]
        r0, rn = o0 * pairs, (o1 - o0) * pairs
        total = own[r0 : r0 + rn, :]
        for dy in range(1, ny):
            y_copy(k, dy).wait_recv()
            total = total + yrecv[dy - 1, r0 : r0 + rn, :].astype(F32)
        dsend[o0:o1] = total.reshape(o1 - o0, pairs, share).astype(BF16)

        def start_d(o, carry):
            d_copy(k, o).start()
            return carry

        if o0 == 0:
            drecv[0] = dsend[0]
        lax.fori_loop(max(o0, 1), o1, start_d, 0)

    for k in range(chunks):
        multiply(k)
        if k == 0:
            drain(gathered.at[i, x, pl.ds(0, nz - 1)], g_send.at[1], g_recv.at[1])
            for dx in range(1, NX):
                g_x_copy(dx).start()
        if k == chunks - 1:
            drain(gathered.at[i, pl.ds(0, NX - 1)], g_send.at[2], g_recv.at[2])
            for dy in range(1, ny):
                g_y_copy(dy).start()
        if k > 0:
            finish(k - 1)
    finish(chunks - 1)

    drain(gathered.at[pl.ds(0, ny - 1)], g_send.at[3], g_recv.at[3])
    for yy in range(ny):
        g_c_copy(yy).start()
    drain(gathered.at[pl.ds(0, ny)], g_send.at[4], g_recv.at[4])

    for b in range(nint):
        for xx in range(NX):
            dress[:, xx, :, b * band : (b + 1) * band] = gathered[b, xx]
    width = dress.shape[-1]
    right = dress[...].reshape(width, width)
    result = jnp.dot(lhs[...], right, preferred_element_type=F32)
    for j in range(vt // 2):
        for ap in range(blocks):
            at = ap * count
            first = result[at : at + count, j * 128 : (j + 1) * 128]
            at += blocks * count
            last = result[at : at + count, j * 128 : (j + 1) * 128]
            cycle[ap, pl.ds(2 * j, count, stride=vt), :] = jnp.where(low, first, pltpu.roll(last, 64, 1))
            cycle[ap, pl.ds(2 * j + 1, count, stride=vt), :] = jnp.where(low, pltpu.roll(first, 64, 1), last)

    for k in range(chunks):
        many(dsend, drecv, d_send, d_recv, k).wait_recv()

    def place(u, carry):
        q = slot_s[u]
        dz = lax.rem(lax.div(q, NX) - z + nz, nz)
        dx = lax.rem(lax.rem(q, NX) - x + NX, NX)
        zi = jnp.where(dz == 0, 0, jnp.where(2 * dz <= nz, 2 * dz - 1, 2 * (nz - dz)))
        block = drecv[zi * NX + dx].astype(F32)
        for b in range(blocks):
            ladder[b, pl.ds(u, pairs, stride=tiles), :] = block[:, b * LANES : (b + 1) * LANES]
        return carry

    lax.fori_loop(0, tiles, place, 0)

    def update(p, carry):
        for a in range(WA):
            at = pl.ds(pl.multiple_of(p * tiles + a * vt, vt), vt)
            below = (pair_energy_s[p] - first_energy[a : a + 1, :]) - second_energy[...]
            for b in range(blocks):
                lanes = slice(b * LANES, (b + 1) * LANES)
                value = amps32[b, at, :] + (ladder[b, at, :] + cycle[b, at, :]) / below[:, lanes]
                out_ref[p, a * vt : (a + 1) * vt, lanes] = value.astype(BF16)
        return carry

    lax.fori_loop(0, pairs, update, 0)

    for k in range(chunks):
        many(asend, arecv, a_send, a_recv, k).wait_send()
        many(dsend, drecv, d_send, d_recv, k).wait_send()
        for yy in range(ny):
            p_copy(k, yy).wait_send()
        for dy in range(1, ny):
            y_copy(k, dy).wait_send()


def shards(
    cuts, amps, amp_mask, integrals, block_mask, in_tiles, out_tiles, vir_energy, pair_energy, dressing
):
    pairs, tiles, share = amps.shape
    npair = tiles
    nz = npair // NX
    nint = integrals.shape[1] // share
    ny = nint // NC
    width = dressing.shape[1]
    chunks = len(cuts) - 1
    every = jnp.arange(tiles, dtype=jnp.int32)
    slot_of = jnp.sum(jnp.where(out_tiles[None, :] == every[:, None], every[None, :], 0), axis=1)
    vmem = pl.BlockSpec(memory_space=pltpu.VMEM)
    smem = pl.BlockSpec(memory_space=pltpu.SMEM)
    dma = pltpu.SemaphoreType.DMA
    total = npair * pairs
    return pl.pallas_call(
        functools.partial(kernel, cuts),
        out_shape=jax.ShapeDtypeStruct(amps.shape, BF16),
        in_specs=[vmem, vmem, pl.BlockSpec(memory_space=pl.ANY), smem, smem, smem, smem, vmem, smem, vmem],
        out_specs=vmem,
        scratch_shapes=[
            pltpu.VMEM((nint * share, share), BF16),
            pltpu.VMEM((share // LANES, pairs * tiles, LANES), F32),
            pltpu.VMEM((npair, pairs, share), BF16),
            pltpu.VMEM((npair, pairs, share), BF16),
            pltpu.VMEM((total, share), BF16),
            pltpu.VMEM((ny, total, share), BF16),
            pltpu.VMEM((ny, total, share), BF16),
            pltpu.VMEM((total, share), F32),
            pltpu.VMEM((ny - 1, total, share), BF16),
            pltpu.VMEM((ny - 1, total, share), BF16),
            pltpu.VMEM((npair, pairs, share), BF16),
            pltpu.VMEM((npair, pairs, share), BF16),
            pltpu.VMEM((nint, NX, nz, dressing.shape[0], width // nint), BF16),
            pltpu.VMEM((nz, NX, dressing.shape[0], width), BF16),
            pltpu.VMEM((pairs * WA * (share // 64), width), BF16),
            pltpu.VMEM((share // LANES, pairs * tiles, LANES), F32),
            pltpu.VMEM((share // LANES, pairs * tiles, LANES), F32),
            pltpu.VMEM((WA, share), F32),
            pltpu.VMEM((tiles // WA, share), F32),
            dma,
            dma((chunks,)),
            dma((chunks,)),
            dma((chunks, ny)),
            dma((chunks, ny)),
            dma((chunks, ny - 1)),
            dma((chunks, ny - 1)),
            dma((chunks,)),
            dma((chunks,)),
            dma((5,)),
            dma((5,)),
        ],
        compiler_params=pltpu.CompilerParams(collective_id=0, has_side_effects=True),
        name="ladder_update",
    )(
        amps, amp_mask, integrals, block_mask, in_tiles, slot_of, vir_energy,
        vir_energy.reshape(-1, 128), pair_energy, dressing,
    )


def solution(mesh):
    npair = mesh.shape["pair"]
    cuts = CUTS if npair == CUTS[-1] else (0, npair // 2, npair)
    in_specs = (
        P("pair", None, "int"),
        P("pair", None),
        P("pair", None, "int"),
        P("pair"),
        P(),
        P(),
        P(),
        P("pair"),
        P("pair", None),
    )
    out_specs = P("pair", None, "int")
    return jax.shard_map(
        functools.partial(shards, cuts), mesh=mesh, in_specs=in_specs, out_specs=out_specs, check_vma=False
    )
```

time: 242 us -> 98.2 us (0.41)
  the two profiles are of different devices: /device:TPU:16 before, /device:TPU:1 now
where the time goes in v1:
time: 98.2 us; the launch traced here: 98 us
  Pallas kernels  94.2 us (96%)
  local copies, waits for them, and re-layouts  1.87 us (2%)
  other arithmetic  1.28 us (1%)
    pallas_call x1, Pallas kernels, shards(): pl.pallas_call(functools.partial(kernel, cuts), out_shape=jax.ShapeDtypeS...  94.2 us

profile of v1, /device:TPU:1, one launch (start us, length us, event | category | flops | bytes accessed | tf_op | source)
XLA Modules:
  0.0 98.0 jit_solution(5661458290472522067)
XLA Ops:
  0.7 1.3 %select_reduce_fusion.slot_s = s32[64]{0:T(128)} fusion(s32[64]{0:T(128)} %param.14), kind=kLoop, calls=%fused_computation | loop fusion | flops 12224 | bytes 512 | tf_op jit(solution)/shard_map/reduce_sum | solution.py:359
  1.9 94.2 %ladder_update.1 = bf16[8,64,512]{2,1,0:T(8,128)(2,1)} custom-call(bf16[8,64,512]{2,1,0:T(8,128)(2,1)} %amps_ref.1, s32[8,64]{1,0:T(8,128)} %mask_ref.1, bf16[1,4096,512]{2,1,0:T(8,128)(2,1)} %ints_hbm.1, s32[1]{0:T(128)S(6)} %copy.11.block_s, s32[64]{0:T(128)} %in_s.1, s32[64]{0:T(128)} %select_reduce_fusion.slot_s, f32[1024]{0:T(1024)} %energy_s.1, ...), custom_call_target="tpu_custom_call" | custom-call | tf_op jit(solution)/shard_map/ladder_update/pallas_call | solution.py:364
  96.2 1.9 %copy.12 = bf16[8,64,512]{2,1,0:T(8,128)(2,1)} copy(bf16[8,64,512]{2,1,0:T(8,128)(2,1)} %ladder_update.1) | data formatting | bytes 1048576

commit v2 on v1

--- a/solution.py
+++ b/solution.py
@@ -13,8 +13,9 @@
 WA = 4
 NX = 4
 LANES = 128
+WINDOW = 2
+LAG = 2
 NC = 2
-CUTS = (0, 44, 64)
 
 
 def kernel(
@@ -24,7 +25,7 @@
     ints_hbm,
     block_s,
     in_s,
-    slot_s,
+    out_s,
     energy_s,
     energy_ref,
     pair_energy_s,
@@ -47,6 +48,7 @@
     lhs,
     cycle,
     ladder,
+    placing,
     first_energy,
     second_energy,
     ints_sem,
@@ -74,13 +76,16 @@
     y, c = lax.div(i, NC), lax.rem(i, NC)
 
     def peer(o, sign):
-        zi, dx = lax.div(o, NX), lax.rem(o, NX)
+        dx, zi = lax.div(o, nz), lax.rem(o, nz)
         half = lax.div(zi + 1, 2)
         dz = jnp.where(lax.rem(zi, 2) == 1, half, nz - half)
         zz = lax.rem(z + nz + sign * dz + nz, nz)
         xx = lax.rem(x + NX + sign * dx, NX)
         return zz * NX + xx
 
+    def far_first(first, last, body):
+        lax.fori_loop(first, last, lambda s, carry: body(last - 1 - (s - first), carry), 0)
+
     def y_peer(dy):
         return lax.rem(y + dy, ny) * NC + c
 
@@ -88,11 +93,14 @@
 
     barrier = pltpu.get_barrier_semaphore()
 
-    def greet(o, carry):
-        pl.semaphore_signal(barrier, 1, device_id={"pair": peer(o, 1)}, device_id_type=MESH)
+    def greet(s, carry):
+        zi, dx = nz - 1 - lax.div(s, NX), lax.rem(s, NX)
+        pl.semaphore_signal(barrier, 1, device_id={"pair": peer(dx * nz + zi, 1)}, device_id_type=MESH)
         return carry
 
-    lax.fori_loop(1, npair, greet, 0)
+    lax.fori_loop(0, npair - NX, greet, 0)
+    for dx in range(1, NX):
+        pl.semaphore_signal(barrier, 1, device_id={"pair": peer(dx * nz, 1)}, device_id_type=MESH)
     pl.semaphore_signal(barrier, 1, device_id={"int": partner}, device_id_type=MESH)
     for dy in range(1, ny):
         pl.semaphore_signal(barrier, 1, device_id={"int": y_peer(dy)}, device_id_type=MESH)
@@ -129,11 +137,15 @@
             src.at[pl.ds(first, last - first)], dst.at[pl.ds(first, last - first)],
             ssem.at[k], rsem.at[k], device_id={"pair": peer(1, 1)}, device_id_type=MESH)
 
-    for k in range(chunks):
-        def start_a(o, carry, k=k):
+    def send_chunk(k):
+        def start_a(o, carry):
             a_copy(k, o).start()
             return carry
-        lax.fori_loop(max(cuts[k], 1), cuts[k + 1], start_a, 0)
+
+        far_first(max(cuts[k], 1), cuts[k + 1], start_a)
+
+    for k in range(min(WINDOW, chunks)):
+        send_chunk(k)
 
     piece = dress_ref.at[:, pl.ds(pl.multiple_of(i * band, band), band)]
     own_piece = pltpu.make_async_copy(piece, gathered.at[i, x, z], g_send.at[0])
@@ -199,6 +211,17 @@
             row = jnp.where(strip == s, energy_s[64 * a + i * (share // 64) + s], row)
         first_energy[a : a + 1, :] = row
 
+    column = lax.broadcasted_iota(jnp.int32, (1, npair * pairs), 1)
+    owner = lax.div(column, pairs)
+
+    def target(o, found):
+        return jnp.where(owner == o, out_s[peer(o, 1)], found)
+
+    row = lax.fori_loop(0, npair, target, jnp.zeros_like(column)) + lax.rem(column, pairs) * tiles
+    for p in range(pairs):
+        own_rows = lax.broadcasted_iota(jnp.int32, (tiles, npair * pairs), 0) + p * tiles
+        placing[p * tiles : (p + 1) * tiles, :] = jnp.where(own_rows == row, 1.0, 0.0).astype(BF16)
+
     scale = block_s[0].astype(F32)
     load_ints.wait()
 
@@ -224,6 +247,8 @@
         o0, o1 = cuts[k], cuts[k + 1]
         r0, rn = o0 * pairs, (o1 - o0) * pairs
         many(asend, arecv, a_send, a_recv, k).wait_recv()
+        if k + WINDOW < chunks:
+            send_chunk(k + WINDOW)
         rows[r0 : r0 + rn, :] = arecv[o0:o1].astype(F32).reshape(rn, share).astype(BF16)
 
         def for_partner(yy, carry):
@@ -273,7 +298,7 @@
 
         if o0 == 0:
             drecv[0] = dsend[0]
-        lax.fori_loop(max(o0, 1), o1, start_d, 0)
+        far_first(max(o0, 1), o1, start_d)
 
     for k in range(chunks):
         multiply(k)
@@ -285,9 +310,10 @@
             drain(gathered.at[i, pl.ds(0, NX - 1)], g_send.at[2], g_recv.at[2])
             for dy in range(1, ny):
                 g_y_copy(dy).start()
-        if k > 0:
-            finish(k - 1)
-    finish(chunks - 1)
+        if k >= LAG:
+            finish(k - LAG)
+    for k in range(max(chunks - LAG, 0), chunks):
+        finish(k)
 
     drain(gathered.at[pl.ds(0, ny - 1)], g_send.at[3], g_recv.at[3])
     for yy in range(ny):
@@ -310,19 +336,11 @@
             cycle[ap, pl.ds(2 * j + 1, count, stride=vt), :] = jnp.where(low, pltpu.roll(first, 64, 1), last)
 
     for k in range(chunks):
+        o0, o1 = cuts[k], cuts[k + 1]
         many(dsend, drecv, d_send, d_recv, k).wait_recv()
-
-    def place(u, carry):
-        q = slot_s[u]
-        dz = lax.rem(lax.div(q, NX) - z + nz, nz)
-        dx = lax.rem(lax.rem(q, NX) - x + NX, NX)
-        zi = jnp.where(dz == 0, 0, jnp.where(2 * dz <= nz, 2 * dz - 1, 2 * (nz - dz)))
-        block = drecv[zi * NX + dx].astype(F32)
-        for b in range(blocks):
-            ladder[b, pl.ds(u, pairs, stride=tiles), :] = block[:, b * LANES : (b + 1) * LANES]
-        return carry
-
-    lax.fori_loop(0, tiles, place, 0)
+        block = drecv[o0:o1].astype(F32).reshape((o1 - o0) * pairs, share).astype(BF16)
+        part = jnp.dot(placing[:, o0 * pairs : o1 * pairs], block, preferred_element_type=F32)
+        ladder[...] = part if k == 0 else ladder[...] + part
 
     def update(p, carry):
         for a in range(WA):
@@ -330,7 +348,7 @@
             below = (pair_energy_s[p] - first_energy[a : a + 1, :]) - second_energy[...]
             for b in range(blocks):
                 lanes = slice(b * LANES, (b + 1) * LANES)
-                value = amps32[b, at, :] + (ladder[b, at, :] + cycle[b, at, :]) / below[:, lanes]
+                value = amps32[b, at, :] + (ladder[at, lanes] + cycle[b, at, :]) / below[:, lanes]
                 out_ref[p, a * vt : (a + 1) * vt, lanes] = value.astype(BF16)
         return carry
 
@@ -355,8 +373,6 @@
     ny = nint // NC
     width = dressing.shape[1]
     chunks = len(cuts) - 1
-    every = jnp.arange(tiles, dtype=jnp.int32)
-    slot_of = jnp.sum(jnp.where(out_tiles[None, :] == every[:, None], every[None, :], 0), axis=1)
     vmem = pl.BlockSpec(memory_space=pltpu.VMEM)
     smem = pl.BlockSpec(memory_space=pltpu.SMEM)
     dma = pltpu.SemaphoreType.DMA
@@ -383,7 +399,8 @@
             pltpu.VMEM((nz, NX, dressing.shape[0], width), BF16),
             pltpu.VMEM((pairs * WA * (share // 64), width), BF16),
             pltpu.VMEM((share // LANES, pairs * tiles, LANES), F32),
-            pltpu.VMEM((share // LANES, pairs * tiles, LANES), F32),
+            pltpu.VMEM((pairs * tiles, share), F32),
+            pltpu.VMEM((pairs * tiles, npair * pairs), BF16),
             pltpu.VMEM((WA, share), F32),
             pltpu.VMEM((tiles // WA, share), F32),
             dma,
@@ -401,14 +418,15 @@
         compiler_params=pltpu.CompilerParams(collective_id=0, has_side_effects=True),
         name="ladder_update",
     )(
-        amps, amp_mask, integrals, block_mask, in_tiles, slot_of, vir_energy,
+        amps, amp_mask, integrals, block_mask, in_tiles, out_tiles, vir_energy,
         vir_energy.reshape(-1, 128), pair_energy, dressing,
     )
 
 
 def solution(mesh):
     npair = mesh.shape["pair"]
-    cuts = CUTS if npair == CUTS[-1] else (0, npair // 2, npair)
+    nz = npair // NX
+    cuts = tuple(range(0, npair + 1, nz))
     in_specs = (
         P("pair", None, "int"),
         P("pair", None),

time: 98.2 us -> 82 us (0.84)
  Pallas kernels: 94.2 us -> 79.3 us
  other arithmetic: 1.28 us -> 0 us
    pallas_call x1, Pallas kernels: 94.2 us -> 79.3 us  [shards(): pl.pallas_call(functools.partial(kernel, cuts), out_shape=jax.ShapeDtypeS...]
    reduce_sum x1 -> x0, other arithmetic: 1.28 us -> none  [shards(): jnp.sum(jnp.where(out_tiles[None, :] == every[:, None], every[None, :], 0...]
where the time goes in v2:
time: 82 us; the launch traced here: 81.8 us
  Pallas kernels  79.3 us (97%)
  local copies, waits for them, and re-layouts  1.87 us (2%)
    pallas_call x1, Pallas kernels, shards(): pl.pallas_call(functools.partial(kernel, cuts), out_shape=jax.ShapeDtypeS...  79.3 us
    unnamed x1, local copies, waits for them, and re-layouts  1.87 us

profile of v2, /device:TPU:1, one launch (start us, length us, event | category | flops | bytes accessed | tf_op | source)
XLA Modules:
  0.0 81.8 jit_solution(5624929027129101300)
XLA Ops:
  0.7 79.3 %ladder_update.1 = bf16[8,64,512]{2,1,0:T(8,128)(2,1)} custom-call(bf16[8,64,512]{2,1,0:T(8,128)(2,1)} %amps_ref.1, s32[8,64]{1,0:T(8,128)} %mask_ref.1, bf16[1,4096,512]{2,1,0:T(8,128)(2,1)} %ints_hbm.1, s32[1]{0:T(128)S(6)} %copy.11.block_s, s32[64]{0:T(128)} %in_s.1, s32[64]{0:T(128)} %out_s.1, f32[1024]{0:T(1024)} %energy_s.1, f32[8,128]{1,0:T(8,128)} %bitcast.1, ...), custom_call_target="tpu_custom_call" | custom-call | tf_op jit(solution)/shard_map/ladder_update/pallas_call | solution.py:380
  80.0 1.9 %copy.12 = bf16[8,64,512]{2,1,0:T(8,128)(2,1)} copy(bf16[8,64,512]{2,1,0:T(8,128)(2,1)} %ladder_update.1) | data formatting | bytes 1048576

commit v3 on v2

--- a/solution.py
+++ b/solution.py
@@ -14,13 +14,14 @@
 NX = 4
 LANES = 128
 WINDOW = 2
+Y_STEP, X_STEP = 1, 2
 LAG = 2
 NC = 2
 
 
 def kernel(
     cuts,
-    amps_ref,
+    amps_hbm,
     mask_ref,
     ints_hbm,
     block_s,
@@ -29,8 +30,10 @@
     energy_s,
     energy_ref,
     pair_energy_s,
+    dress_hbm,
+    out_ref,
+    amps_ref,
     dress_ref,
-    out_ref,
     ints,
     amps32,
     asend,
@@ -52,6 +55,8 @@
     first_energy,
     second_energy,
     ints_sem,
+    amps_sem,
+    dress_sem,
     a_send,
     a_recv,
     p_send,
@@ -66,8 +71,7 @@
     npair = asend.shape[0]
     pairs, tiles, share = amps_ref.shape
     nz = npair // NX
-    nint, _, _, _, band = gathered.shape
-    ny = nint // NC
+    _, _, ny, _, _, band = gathered.shape
     vt = tiles // WA
     chunks = len(cuts) - 1
     blocks = share // LANES
@@ -105,8 +109,13 @@
     for dy in range(1, ny):
         pl.semaphore_signal(barrier, 1, device_id={"int": y_peer(dy)}, device_id_type=MESH)
 
+    load_amps = pltpu.make_async_copy(amps_hbm, amps_ref, amps_sem)
+    load_amps.start()
+    load_dress = pltpu.make_async_copy(dress_hbm, dress_ref, dress_sem)
+    load_dress.start()
     load_ints = pltpu.make_async_copy(ints_hbm.at[0], ints, ints_sem)
     load_ints.start()
+    load_amps.wait()
 
     mask_t = jnp.transpose(mask_ref[...].astype(F32))
     for p in range(pairs):
@@ -148,28 +157,29 @@
         send_chunk(k)
 
     piece = dress_ref.at[:, pl.ds(pl.multiple_of(i * band, band), band)]
-    own_piece = pltpu.make_async_copy(piece, gathered.at[i, x, z], g_send.at[0])
+    own_piece = pltpu.make_async_copy(piece, gathered.at[x, c, y, z], g_send.at[0])
+    load_dress.wait()
     own_piece.start()
     own_piece.wait()
 
     def g_z_copy(dz):
         return pltpu.make_async_remote_copy(
-            piece, gathered.at[i, x, z], g_send.at[1], g_recv.at[1],
+            piece, gathered.at[x, c, y, z], g_send.at[1], g_recv.at[1],
             device_id={"pair": lax.rem(z + dz, nz) * NX + x}, device_id_type=MESH)
 
     def g_x_copy(dx):
         return pltpu.make_async_remote_copy(
-            gathered.at[i, x], gathered.at[i, x], g_send.at[2], g_recv.at[2],
+            gathered.at[x, c], gathered.at[x, c], g_send.at[3], g_recv.at[3],
             device_id={"pair": z * NX + lax.rem(x + dx, NX)}, device_id_type=MESH)
 
     def g_y_copy(dy):
         return pltpu.make_async_remote_copy(
-            gathered.at[i], gathered.at[i], g_send.at[3], g_recv.at[3],
+            gathered.at[x, c, y], gathered.at[x, c, y], g_send.at[2], g_recv.at[2],
             device_id={"int": y_peer(dy)}, device_id_type=MESH)
 
-    def g_c_copy(yy):
-        return pltpu.make_async_remote_copy(
-            gathered.at[yy * NC + c], gathered.at[yy * NC + c], g_send.at[4], g_recv.at[4],
+    def g_c_copy(xx):
+        return pltpu.make_async_remote_copy(
+            gathered.at[xx, c], gathered.at[xx, c], g_send.at[4], g_recv.at[4],
             device_id={"int": partner}, device_id_type=MESH)
 
     def start_gz(dz, carry):
@@ -302,27 +312,27 @@
 
     for k in range(chunks):
         multiply(k)
-        if k == 0:
-            drain(gathered.at[i, x, pl.ds(0, nz - 1)], g_send.at[1], g_recv.at[1])
+        if k >= LAG:
+            finish(k - LAG)
+        if k == Y_STEP:
+            drain(gathered.at[x, c, y, pl.ds(0, nz - 1)], g_send.at[1], g_recv.at[1])
+            for dy in range(1, ny):
+                g_y_copy(dy).start()
+        if k == X_STEP:
+            drain(gathered.at[x, c, pl.ds(0, ny - 1)], g_send.at[2], g_recv.at[2])
             for dx in range(1, NX):
                 g_x_copy(dx).start()
-        if k == chunks - 1:
-            drain(gathered.at[i, pl.ds(0, NX - 1)], g_send.at[2], g_recv.at[2])
-            for dy in range(1, ny):
-                g_y_copy(dy).start()
-        if k >= LAG:
-            finish(k - LAG)
     for k in range(max(chunks - LAG, 0), chunks):
         finish(k)
-
-    drain(gathered.at[pl.ds(0, ny - 1)], g_send.at[3], g_recv.at[3])
-    for yy in range(ny):
-        g_c_copy(yy).start()
-    drain(gathered.at[pl.ds(0, ny)], g_send.at[4], g_recv.at[4])
-
-    for b in range(nint):
-        for xx in range(NX):
-            dress[:, xx, :, b * band : (b + 1) * band] = gathered[b, xx]
+    drain(gathered.at[pl.ds(0, NX - 1), c], g_send.at[3], g_recv.at[3])
+    for xx in range(NX):
+        g_c_copy(xx).start()
+    drain(gathered.at[:, c], g_send.at[4], g_recv.at[4])
+    for xx in range(NX):
+        for cc in range(NC):
+            for yy in range(ny):
+                b = yy * NC + cc
+                dress[:, xx, :, b * band : (b + 1) * band] = gathered[xx, cc, yy]
     width = dress.shape[-1]
     right = dress[...].reshape(width, width)
     result = jnp.dot(lhs[...], right, preferred_element_type=F32)
@@ -375,14 +385,17 @@
     chunks = len(cuts) - 1
     vmem = pl.BlockSpec(memory_space=pltpu.VMEM)
     smem = pl.BlockSpec(memory_space=pltpu.SMEM)
+    hbm = pl.BlockSpec(memory_space=pl.ANY)
     dma = pltpu.SemaphoreType.DMA
     total = npair * pairs
     return pl.pallas_call(
         functools.partial(kernel, cuts),
         out_shape=jax.ShapeDtypeStruct(amps.shape, BF16),
-        in_specs=[vmem, vmem, pl.BlockSpec(memory_space=pl.ANY), smem, smem, smem, smem, vmem, smem, vmem],
+        in_specs=[hbm, vmem, hbm, smem, smem, smem, smem, vmem, smem, hbm],
         out_specs=vmem,
         scratch_shapes=[
+            pltpu.VMEM(amps.shape, BF16),
+            pltpu.VMEM(dressing.shape, BF16),
             pltpu.VMEM((nint * share, share), BF16),
             pltpu.VMEM((share // LANES, pairs * tiles, LANES), F32),
             pltpu.VMEM((npair, pairs, share), BF16),
@@ -395,7 +408,7 @@
             pltpu.VMEM((ny - 1, total, share), BF16),
             pltpu.VMEM((npair, pairs, share), BF16),
             pltpu.VMEM((npair, pairs, share), BF16),
-            pltpu.VMEM((nint, NX, nz, dressing.shape[0], width // nint), BF16),
+            pltpu.VMEM((NX, NC, ny, nz, dressing.shape[0], width // nint), BF16),
             pltpu.VMEM((nz, NX, dressing.shape[0], width), BF16),
             pltpu.VMEM((pairs * WA * (share // 64), width), BF16),
             pltpu.VMEM((share // LANES, pairs * tiles, LANES), F32),
@@ -403,6 +416,8 @@
             pltpu.VMEM((pairs * tiles, npair * pairs), BF16),
             pltpu.VMEM((WA, share), F32),
             pltpu.VMEM((tiles // WA, share), F32),
+            dma,
+            dma,
             dma,
             dma((chunks,)),
             dma((chunks,)),

time: 82 us -> 79.3 us (0.967)
  Pallas kernels: 79.3 us -> 76.5 us
    pallas_call x1, Pallas kernels: 79.3 us -> 76.5 us  [shards(): pl.pallas_call(functools.partial(kernel, cuts), out_shape=jax.ShapeDtypeS...]
where the time goes in v3:
time: 79.3 us; the launch traced here: 79.1 us
  Pallas kernels  76.5 us (96%)
  local copies, waits for them, and re-layouts  1.87 us (2%)
    pallas_call x1, Pallas kernels, shards(): pl.pallas_call(functools.partial(kernel, cuts), out_shape=jax.ShapeDtypeS...  76.5 us
    unnamed x1, local copies, waits for them, and re-layouts  1.87 us

profile of v3, /device:TPU:1, one launch (start us, length us, event | category | flops | bytes accessed | tf_op | source)
XLA Modules:
  0.0 79.1 jit_solution(5521476892123805050)
XLA Ops:
  0.7 76.5 %ladder_update.1 = bf16[8,64,512]{2,1,0:T(8,128)(2,1)} custom-call(bf16[8,64,512]{2,1,0:T(8,128)(2,1)} %amps_hbm.1, s32[8,64]{1,0:T(8,128)} %mask_ref.1, bf16[1,4096,512]{2,1,0:T(8,128)(2,1)} %ints_hbm.1, s32[1]{0:T(128)S(6)} %copy.11.block_s, s32[64]{0:T(128)} %in_s.1, s32[64]{0:T(128)} %out_s.1, f32[1024]{0:T(1024)} %energy_s.1, f32[8,128]{1,0:T(8,128)} %bitcast.1, ...), custom_call_target="tpu_custom_call" | custom-call | tf_op jit(solution)/shard_map/ladder_update/pallas_call | solution.py:391
  77.2 1.9 %copy.12 = bf16[8,64,512]{2,1,0:T(8,128)(2,1)} copy(bf16[8,64,512]{2,1,0:T(8,128)(2,1)} %ladder_update.1) | data formatting | bytes 1048576

commit v4 on v3

--- a/solution.py
+++ b/solution.py
@@ -261,7 +261,8 @@
             send_chunk(k + WINDOW)
         rows[r0 : r0 + rn, :] = arecv[o0:o1].astype(F32).reshape(rn, share).astype(BF16)
 
-        def for_partner(yy, carry):
+        def for_partner(step, carry):
+            yy = lax.rem(y + ny - 1 - step, ny)
             psend[yy, r0 : r0 + rn, :] = product(r0, rn, yy * NC + 1 - c)
             p_copy(k, yy).start()
             return carry

time: 79.3 us -> 78.1 us (0.985)
  Pallas kernels: 76.5 us -> 75.4 us
    pallas_call x1, Pallas kernels: 76.5 us -> 75.4 us  [shards(): pl.pallas_call(functools.partial(kernel, cuts), out_shape=jax.ShapeDtypeS...]
where the time goes in v4:
time: 78.1 us; the launch traced here: 77.9 us
  Pallas kernels  75.4 us (97%)
  local copies, waits for them, and re-layouts  1.87 us (2%)
    pallas_call x1, Pallas kernels, shards(): pl.pallas_call(functools.partial(kernel, cuts), out_shape=jax.ShapeDtypeS...  75.4 us
    unnamed x1, local copies, waits for them, and re-layouts  1.87 us

profile of v4, /device:TPU:1, one launch (start us, length us, event | category | flops | bytes accessed | tf_op | source)
XLA Modules:
  0.0 77.9 jit_solution(5638593955311001552)
XLA Ops:
  0.7 75.4 %ladder_update.1 = bf16[8,64,512]{2,1,0:T(8,128)(2,1)} custom-call(bf16[8,64,512]{2,1,0:T(8,128)(2,1)} %amps_hbm.1, s32[8,64]{1,0:T(8,128)} %mask_ref.1, bf16[1,4096,512]{2,1,0:T(8,128)(2,1)} %ints_hbm.1, s32[1]{0:T(128)S(6)} %copy.11.block_s, s32[64]{0:T(128)} %in_s.1, s32[64]{0:T(128)} %out_s.1, f32[1024]{0:T(1024)} %energy_s.1, f32[8,128]{1,0:T(8,128)} %bitcast.1, ...), custom_call_target="tpu_custom_call" | custom-call | tf_op jit(solution)/shard_map/ladder_update/pallas_call | solution.py:392
  76.1 1.9 %copy.12 = bf16[8,64,512]{2,1,0:T(8,128)(2,1)} copy(bf16[8,64,512]{2,1,0:T(8,128)(2,1)} %ladder_update.1) | data formatting | bytes 1048576

commit v5 on v4

--- a/solution.py
+++ b/solution.py
@@ -93,6 +93,10 @@
     def y_peer(dy):
         return lax.rem(y + dy, ny) * NC + c
 
+    def turn(step):
+        dy = ny - 1 - step
+        return jnp.where(dy == ny - 1, ny // 2, jnp.where(dy == ny // 2, ny - 1, dy))
+
     partner = y * NC + (1 - c)
 
     barrier = pltpu.get_barrier_semaphore()
@@ -262,7 +266,7 @@
         rows[r0 : r0 + rn, :] = arecv[o0:o1].astype(F32).reshape(rn, share).astype(BF16)
 
         def for_partner(step, carry):
-            yy = lax.rem(y + ny - 1 - step, ny)
+            yy = lax.rem(y + turn(step), ny)
             psend[yy, r0 : r0 + rn, :] = product(r0, rn, yy * NC + 1 - c)
             p_copy(k, yy).start()
             return carry
@@ -270,7 +274,7 @@
         lax.fori_loop(0, ny, for_partner, 0)
 
         def for_chip(step, carry):
-            dy = ny - 1 - step
+            dy = turn(step)
             yy = lax.rem(y + dy, ny)
             part = product(r0, rn, yy * NC + c).astype(F32)
             p_copy(k, yy).wait_recv()

time: 78.1 us -> 78.1 us (level)
  no operation moved by 1% of the time
where the time goes in v5:
time: 78.1 us; the launch traced here: 77.9 us
  Pallas kernels  75.4 us (97%)
  local copies, waits for them, and re-layouts  1.87 us (2%)
    pallas_call x1, Pallas kernels, shards(): pl.pallas_call(functools.partial(kernel, cuts), out_shape=jax.ShapeDtypeS...  75.4 us
    unnamed x1, local copies, waits for them, and re-layouts  1.87 us

profile of v5, /device:TPU:1, one launch (start us, length us, event | category | flops | bytes accessed | tf_op | source)
XLA Modules:
  0.0 77.9 jit_solution(13037465585807334394)
XLA Ops:
  0.7 75.4 %ladder_update.1 = bf16[8,64,512]{2,1,0:T(8,128)(2,1)} custom-call(bf16[8,64,512]{2,1,0:T(8,128)(2,1)} %amps_hbm.1, s32[8,64]{1,0:T(8,128)} %mask_ref.1, bf16[1,4096,512]{2,1,0:T(8,128)(2,1)} %ints_hbm.1, s32[1]{0:T(128)S(6)} %copy.11.block_s, s32[64]{0:T(128)} %in_s.1, s32[64]{0:T(128)} %out_s.1, f32[1024]{0:T(1024)} %energy_s.1, f32[8,128]{1,0:T(8,128)} %bitcast.1, ...), custom_call_target="tpu_custom_call" | custom-call | tf_op jit(solution)/shard_map/ladder_update/pallas_call | solution.py:396
  76.0 1.9 %copy.12 = bf16[8,64,512]{2,1,0:T(8,128)(2,1)} copy(bf16[8,64,512]{2,1,0:T(8,128)(2,1)} %ladder_update.1) | data formatting | bytes 1048576
